TPU v7x, 32 devices: a whole 2x2x4 slice. The times are simulated.
32 devices in a mesh: groups: 2 (over x), ctx: 16 (over z, y, core).
Axes of the slice: x: 2, y: 2, z: 4, core: 2. Of those that a mesh axis runs over, the one named last changes fastest.
Arguments:
- signal_spectrum: bfloat16 [2, 8192, 4096], P(None, ('groups', 'ctx')), parts along dimension 1, may hold values from -6 to 6
- filter_spectrum: bfloat16 [2, 4096, 4096], P(None, 'ctx'), may hold values from -6 to 6
- output_gate: bfloat16 [4096, 4096], P(('groups', 'ctx')), parts along dimension 0, may hold values from -8 to 8
- projection: bfloat16 [4096, 384], replicated, may hold values from -0.5 to 0.5
Outputs:
- attended: bfloat16 [4096, 128], P(('groups', 'ctx')), parts along dimension 0
There are 2 independent parts, one for each index of `groups`. A program takes and returns all parts, laid end to end along the dimension named above; an argument that names none is the same for every part. Nothing has to cross between parts.
All inputs are finite; a program needn't handle non-finite values.
Results may differ from a plain program's by a relative error of at most 0.019.
Values may be sent and summed in bfloat16 or wider, within the bound.
No kernel may reach another device: no remote copies, remote signals or barrier semaphores. Data moves between devices by JAX's collectives and lax.ppermute only.
A program may use at most 128 MiB of HBM per device.

v0:
```python
import math
import jax
import jax.numpy as jnp
from jax import lax
from jax.sharding import PartitionSpec as P

TWO_PI = 2.0 * math.pi
FLOOR = -1e30
HIGHEST = lax.Precision.HIGHEST


def unit_circle(numerator, modulus):
    phases = TWO_PI / modulus * numerator.astype(jnp.float32)
    return (jnp.cos(phases), jnp.sin(phases))


def across_sources(pieces, span_total):
    sources = pieces.shape[2]
    freq_count = pieces.shape[3]
    form = "ud,cdp->cup"
    ordinal = jnp.arange(sources, dtype=jnp.int32)
    cos_table, sin_table = unit_circle(ordinal[:, None] * ordinal[None, :] % sources, sources)
    real_mid = jnp.einsum(form, cos_table, pieces[0], precision=HIGHEST) - jnp.einsum(
        form, sin_table, pieces[1], precision=HIGHEST
    )
    imag_mid = jnp.einsum(form, sin_table, pieces[0], precision=HIGHEST) + jnp.einsum(
        form, cos_table, pieces[1], precision=HIGHEST
    )
    freq_ids = jnp.arange(freq_count, dtype=jnp.int32)
    turn_cos, turn_sin = unit_circle(ordinal[:, None] * freq_ids[None, :] % span_total, span_total)
    turn_cos = turn_cos[None, :, :]
    turn_sin = turn_sin[None, :, :]
    real_out = real_mid * turn_cos - imag_mid * turn_sin
    imag_out = real_mid * turn_sin + imag_mid * turn_cos
    return jnp.stack([real_out, imag_out])


def across_freqs(pieces, out_rows, freq_count, span_total, form):
    row_ids = jnp.arange(out_rows, dtype=jnp.int32)
    freq_ids = jnp.arange(freq_count, dtype=jnp.int32)
    cos_table, sin_table = unit_circle(
        row_ids[:, None] * freq_ids[None, :] % freq_count, freq_count
    )
    result = jnp.einsum(form, cos_table, pieces[0], precision=HIGHEST) - jnp.einsum(
        form, sin_table, pieces[1], precision=HIGHEST
    )
    return result * (1.0 / math.sqrt(span_total))


def per_device(signal_spectrum, filter_spectrum, output_gate, projection):
    axis_count = lax.axis_size("ctx")
    me_index = lax.axis_index("ctx")
    rows_dev = output_gate.shape[0]
    freqs_dev = signal_spectrum.shape[1]
    span_total = axis_count * freqs_dev
    head_size = projection.shape[1] // 3
    local_rows = jnp.arange(rows_dev, dtype=jnp.int32)
    query_pos = me_index * rows_dev + local_rows
    signal = signal_spectrum.astype(jnp.float32)
    kernel = filter_spectrum.astype(jnp.float32)
    product = jnp.stack(
        [
            signal[0] * kernel[0] - signal[1] * kernel[1],
            signal[0] * kernel[1] + signal[1] * kernel[0],
        ]
    )
    chan_count = product.shape[2] // axis_count
    turned = jnp.swapaxes(product, 1, 2)
    gathered_freqs = lax.all_to_all(turned, "ctx", split_axis=1, concat_axis=2, tiled=True)
    pieces = gathered_freqs.reshape(2, chan_count, axis_count, freqs_dev)
    spread = across_sources(pieces, span_total)
    form = "vp,cup->vuc"
    mixed_rows = across_freqs(spread, rows_dev, freqs_dev, span_total, form)
    mixed_rows = lax.all_to_all(
        mixed_rows.reshape(axis_count, rows_dev, chan_count),
        "ctx",
        split_axis=0,
        concat_axis=2,
        tiled=True,
    ).reshape(rows_dev, -1)
    gated = (mixed_rows * output_gate.astype(jnp.float32)).astype(jnp.bfloat16)
    packed = jnp.dot(gated, projection, preferred_element_type=jnp.float32)
    query_rows = packed[:, :head_size].astype(jnp.bfloat16)
    key_rows = packed[:, head_size : 2 * head_size].astype(jnp.bfloat16)
    value_rows = packed[:, 2 * head_size :].astype(jnp.bfloat16)
    score_scale = 1.0 / math.sqrt(head_size)
    top_query = jnp.max(query_pos)

    def absorb_block(carried, key_part, value_part, first_key):
        key_index = first_key + jnp.arange(key_part.shape[0], dtype=jnp.int32)

        def update(current):
            running_max, totals, weighted = current
            scores = (
                jnp.einsum("qh,kh->qk", query_rows, key_part, preferred_element_type=jnp.float32)
                * score_scale
            )
            allowed = key_index[None, :] <= query_pos[:, None]
            scores = jnp.where(allowed, scores, FLOOR)
            new_max = jnp.maximum(running_max, jnp.max(scores, axis=1))
            exponents = jnp.where(allowed, jnp.exp(scores - new_max[:, None]), 0.0)
            factor = jnp.exp(running_max - new_max)
            totals = totals * factor + jnp.sum(exponents, axis=1)
            weighted = weighted * factor[:, None] + jnp.dot(
                exponents.astype(jnp.bfloat16), value_part, preferred_element_type=jnp.float32
            )
            return (new_max, totals, weighted)

        def unchanged(current):
            return current

        return lax.cond(jnp.min(key_index) > top_query, unchanged, update, carried)

    def absorb(carried, pieces, first_row):
        key_part, value_part = pieces
        key_total = key_part.shape[0]
        block_rows = 2048 if key_total > 2048 and key_total % 2048 == 0 else key_total
        if block_rows == key_total:
            return absorb_block(carried, key_part, value_part, first_row)
        block_count = key_total // block_rows
        key_blocks = key_part.reshape(block_count, block_rows, -1)
        value_blocks = value_part.reshape(block_count, block_rows, -1)
        offsets = first_row + block_rows * jnp.arange(block_count, dtype=jnp.int32)

        def step_block(current, inputs):
            return (absorb_block(current, inputs[0], inputs[1], inputs[2]), None)

        final_state, unused = lax.scan(step_block, carried, (key_blocks, value_blocks, offsets))
        return final_state

    initial = (
        jnp.full((rows_dev,), FLOOR, jnp.float32),
        jnp.zeros((rows_dev,), jnp.float32),
        jnp.zeros((rows_dev, head_size), jnp.float32),
    )
    running_max, totals, weighted = absorb(
        initial,
        (
            lax.all_gather(key_rows, "ctx", axis=0, tiled=True),
            lax.all_gather(value_rows, "ctx", axis=0, tiled=True),
        ),
        jnp.int32(0),
    )
    attended = (weighted / totals[:, None]).astype(jnp.bfloat16)
    return attended


def solution(mesh):
    in_specs = (
        P(None, ("groups", "ctx"), None),
        P(None, "ctx", None),
        P(("groups", "ctx"), None),
        P(),
    )
    out_specs = P(("groups", "ctx"), None)
    return jax.shard_map(
        per_device, mesh=mesh, in_specs=in_specs, out_specs=out_specs, check_vma=False
    )
```

profile of v0, /device:TPU:0, one launch (start us, length us, event | category | flops | bytes accessed | tf_op | source)
XLA Modules:
  0.0 387.8 jit_solution(934145070185385344)
XLA Ops:
  0.0 11.3 %copy.21 = bf16[2,256,4096]{1,0,2:T(2,128)(2,1)} copy(bf16[2,256,4096]{2,1,0:T(8,128)(2,1)} %param.6) | data formatting | bytes 8388608 | tf_op args[0]
  11.3 6.6 %convert_element_type.55 = f32[2,256,4096]{1,0,2:T(2,128)} convert(bf16[2,256,4096]{1,0,2:T(2,128)(2,1)} %copy.21) | non-fusion elementwise | flops 2097152 | bytes 12582912 | tf_op jit(solution)/shard_map/convert_element_type | solution.py:59
  17.9 11.1 %copy.22 = bf16[2,256,4096]{1,0,2:T(2,128)(2,1)} copy(bf16[2,256,4096]{2,1,0:T(8,128)(2,1)} %param.7) | data formatting | bytes 8388608 | tf_op args[1]
  29.1 5.2 %convert_element_type.56 = f32[2,256,4096]{1,0,2:T(2,128)S(1)} convert(bf16[2,256,4096]{1,0,2:T(2,128)(2,1)} %copy.22) | non-fusion elementwise | flops 2097152 | bytes 12582912 | tf_op jit(solution)/shard_map/convert_element_type | solution.py:60
  34.2 0.0 copy-done.1
  34.2 10.9 %multiply_subtract_fusion = (f32[1,256,4096]{1,0,2:T(1,128)S(1)}, f32[1,256,4096]{1,0,2:T(1,128)S(1)}) fusion(f32[2,256,4096]{1,0,2:T(2,128)S(1)} %convert_element_type.56, f32[2,256,4096]{1,0,2:T(2,128)S(1)} %copy-done.1), kind=kLoop, calls=%fused_computation.30 | loop fusion | flops 6291456 | bytes 25165824 | tf_op jit(solution)/shard_map/sub | solution.py:63
  45.2 8.7 %maximum_bitcast_fusion = f32[2,4096,256]{2,0,1:T(2,128)} fusion(f32[1,256,4096]{1,0,2:T(1,128)S(1)} %get-tuple-element.30, f32[1,256,4096]{1,0,2:T(1,128)S(1)} %get-tuple-element.29), kind=kLoop, calls=%fused_computation.15 | loop fusion | flops 2097152 | bytes 16777216 | tf_op jit(solution)/shard_map/transpose | solution.py:68
  53.9 8.0 %all-to-all-start = ((f32[2,4096,256]{2,0,1:T(2,128)}), f32[2,4096,256]{2,0,1:T(2,128)}, u32[]{:S(2)}, u32[]{:S(2)}) async-start(f32[2,4096,256]{2,0,1:T(2,128)} %maximum_bitcast_fusion), calls=%async_computation | async-start | bytes 16777216 | tf_op jit(solution)/shard_map/all_to_all | solution.py:69
  61.9 0.1 fusion.51
  62.0 150.0 %all-to-all-done = f32[2,4096,256]{2,0,1:T(2,128)} async-done(((f32[2,4096,256]{2,0,1:T(2,128)}), f32[2,4096,256]{2,0,1:T(2,128)}, u32[]{:S(2)}, u32[]{:S(2)}) %all-to-all-start) | async-done | bytes 8388640 | tf_op jit(solution)/shard_map/all_to_all | solution.py:69
  212.0 8.2 %copy.39 = f32[2,16,256,256]{3,1,2,0:T(8,128)S(1)} copy(f32[2,16,256,256]{3,0,2,1:T(2,128)} %bitcast.1) | data formatting | bytes 16777216 | tf_op jit(solution)/shard_map/all_to_all | solution.py:69
  220.2 4.1 %fusion.18 = f32[256,256,16]{1,2,0:T(8,128)S(1)} fusion(f32[2,256,16,256]{3,2,1,0:T(8,128)S(1)} %bitcast.66), kind=kOutput, calls=%fused_computation.32 | convolution fusion | flops 201330176 | bytes 8388608 | tf_op jit(solution)/shard_map/ud,cdp->cup/dot_general | solution.py:23
  224.3 4.3 %fusion.17 = f32[256,256,16]{1,2,0:T(8,128)S(1)} fusion(f32[2,256,16,256]{3,2,1,0:T(8,128)S(1)} %bitcast.67), kind=kOutput, calls=%fused_computation.31 | convolution fusion | flops 201330176 | bytes 8388608 | tf_op jit(solution)/shard_map/ud,cdp->cup/dot_general | solution.py:26
  228.6 4.1 %fusion.21 = f32[256,256,16]{1,2,0:T(8,128)S(1)} fusion(f32[256,256,16]{1,2,0:T(8,128)S(1)} %fusion.18, f32[2,256,16,256]{3,2,1,0:T(8,128)S(1)} %bitcast.68), kind=kOutput, calls=%fused_computation.35 | convolution fusion | flops 202378752 | bytes 12582912 | tf_op jit(solution)/shard_map/ud,cdp->cup/dot_general | solution.py:23
  232.7 5.1 %fusion.11 = (f32[256,16,256]{2,1,0:T(8,128)S(1)}, f32[256,16,256]{2,1,0:T(8,128)S(1)}) fusion(f32[256,256,16]{1,2,0:T(8,128)S(1)} %fusion.21, f32[16,256]{1,0:T(8,128)S(1)} %get-tuple-element.35, f32[16,256]{1,0:T(8,128)S(1)} %get-tuple-element.36, f32[256,256,16]{1,2,0:T(8,128)S(1)} %fusion.17, f32[2,256,16,256]{3,2,1,0:T(8,128)S(1)} %bitcast.69), kind=kOutput, calls=%fused_computation.21 | convolution fusion | flops 208670208 | bytes 21004288 | tf_op jit(solution)/shard_map/ud,cdp->cup/dot_general | solution.py:26
  237.8 7.4 %fusion.13 = f32[256,16,128]{0,2,1:T(8,128)S(1)} fusion(f32[256,16,256]{2,1,0:T(8,128)S(1)} %get-tuple-element.32), kind=kOutput, calls=%fused_computation.25 | convolution fusion | flops 1611071488 | bytes 6291456 | tf_op jit(solution)/shard_map/vp,cup->vuc/dot_general | solution.py:44
  245.3 7.3 %multiply_bitcast_fusion = f32[128,16,256]{2,0,1:T(8,128)S(1)} fusion(f32[256,16,128]{0,2,1:T(8,128)S(1)} %fusion.13, f32[256,16,256]{2,1,0:T(8,128)S(1)} %get-tuple-element.31), kind=kOutput, calls=%fused_computation.39 | convolution fusion | flops 1612120064 | bytes 8388608 | tf_op jit(solution)/shard_map/vp,cup->vuc/dot_general | solution.py:44
  252.5 2.5 copy.27
  255.0 36.5 %all-to-all-start.1 = ((f32[16,128,256]{2,1,0:T(8,128)}), f32[16,128,256]{2,1,0:T(8,128)}, u32[]{:S(2)}, u32[]{:S(2)}) async-start(f32[16,128,256]{2,1,0:T(8,128)} %bitcast.70), calls=%async_computation.1 | async-start | bytes 4194304 | tf_op jit(solution)/shard_map/all_to_all | solution.py:74
  291.6 2.3 copy.29
  293.9 0.6 fusion.86
  295.2 37.5 %all-to-all-done.1 = f32[16,128,256]{2,1,0:T(8,128)} async-done(((f32[16,128,256]{2,1,0:T(8,128)}), f32[16,128,256]{2,1,0:T(8,128)}, u32[]{:S(2)}, u32[]{:S(2)}) %all-to-all-start.1) | async-done | bytes 2097184 | tf_op jit(solution)/shard_map/all_to_all | solution.py:74
  332.6 2.9 copy.28
  335.5 2.1 fusion.23
  337.6 0.8 convolution_convert_fusion
  338.3 28.5 %all_gather.6 = bf16[2048,128]{1,0:T(8,128)(2,1)S(1)} all-gather(bf16[128,128]{1,0:T(8,128)(2,1)S(1)} %get-tuple-element.34), channel_id=1, replica_groups=mesh['groups'=2,'ctx'=16] {'ctx'}, dimensions={0}, use_global_device_ids=true | all-gather | bytes 557056 | tf_op jit(solution)/shard_map/all_gather | solution.py:139
  366.8 18.9 %all_gather.7 = bf16[2048,128]{1,0:T(8,128)(2,1)S(1)} all-gather(bf16[128,128]{1,0:T(8,128)(2,1)S(1)} %get-tuple-element.33), channel_id=1, replica_groups=mesh['groups'=2,'ctx'=16] {'ctx'}, dimensions={0}, use_global_device_ids=true | all-gather | bytes 557056 | tf_op jit(solution)/shard_map/all_gather | solution.py:140
  385.7 1.2 conditional.1
  385.7 0.4 fusion.87
  386.1 0.4 fusion.2
  386.4 0.4 convolution_add_fusion
  386.8 0.7 divide_convert_fusion
  (8 shorter events, 0.0 us)
Async XLA Ops:
  0.0 337.6 %copy-start = (bf16[4096,384]{1,0:T(8,128)(2,1)S(1)}, bf16[4096,384]{1,0:T(8,128)(2,1)}, u32[]{:S(2)}) copy-start(bf16[4096,384]{1,0:T(8,128)(2,1)} %param.9) | copy-start | bytes 9437188
  29.1 5.2 %copy-start.1 = (f32[2,256,4096]{1,0,2:T(2,128)S(1)}, f32[2,256,4096]{1,0,2:T(2,128)}, u32[]{:S(2)}) copy-start(f32[2,256,4096]{1,0,2:T(2,128)} %convert_element_type.55) | copy-start | bytes 25165828
  53.9 158.0 %all-to-all-start = ((f32[2,4096,256]{2,0,1:T(2,128)}), f32[2,4096,256]{2,0,1:T(2,128)}, u32[]{:S(2)}, u32[]{:S(2)}) async-start(f32[2,4096,256]{2,0,1:T(2,128)} %maximum_bitcast_fusion), calls=%async_computation | async-start | bytes 16777216 | tf_op jit(solution)/shard_map/all_to_all | solution.py:69
  255.0 77.6 %all-to-all-start.1 = ((f32[16,128,256]{2,1,0:T(8,128)}), f32[16,128,256]{2,1,0:T(8,128)}, u32[]{:S(2)}, u32[]{:S(2)}) async-start(f32[16,128,256]{2,1,0:T(8,128)} %bitcast.70), calls=%async_computation.1 | async-start | bytes 4194304 | tf_op jit(solution)/shard_map/all_to_all | solution.py:74
where the time goes:
time: 392 us; the launch traced here: 388 us
  waiting for transfers between devices  187 us (48%)
  blocking collectives  47.3 us (12%)
  starting transfers between devices  44.5 us (11%)
  local copies, waits for them, and re-layouts  38.4 us (10%)
  other arithmetic  35.3 us (9%)
  matrix products  33.8 us (9%)
    all_to_all x1, waiting for transfers between devices, per_device(): lax.all_to_all(turned, 'ctx', split_axis=1, concat_axis=2, tiled=True)  150 us
    all_to_all x1, waiting for transfers between devices, per_device(): lax.all_to_all(mixed_rows.reshape(axis_count, rows_dev, chan_count), 'ctx...  37.5 us
    all_to_all x1, starting transfers between devices, per_device(): lax.all_to_all(mixed_rows.reshape(axis_count, rows_dev, chan_count), 'ctx...  36.5 us
    all_gather x1, blocking collectives, per_device(): lax.all_gather(key_rows, 'ctx', axis=0, tiled=True)  28.5 us
    unnamed x7, local copies, waits for them, and re-layouts  24.7 us
    all_gather x1, blocking collectives, per_device(): lax.all_gather(value_rows, 'ctx', axis=0, tiled=True)  18.9 us
    sub x1, other arithmetic, per_device(): signal[0] * kernel[0] - signal[1] * kernel[1]  10.9 us
    transpose x1, other arithmetic, per_device(): turned = jnp.swapaxes(product, 1, 2)  8.75 us
  transfers between devices with their start and end apart: 2, of which 2 were waited for; matrix products, arithmetic and copies ran while one was open for 1% of the time, Pallas kernels for 0%

commit v1 on v0

--- a/solution.py
+++ b/solution.py
@@ -7,6 +7,18 @@
 TWO_PI = 2.0 * math.pi
 FLOOR = -1e30
 HIGHEST = lax.Precision.HIGHEST
+
+
+def ring_gather(value, axis, dim):
+    ways, here, step = (lax.axis_size(axis), lax.axis_index(axis), value.shape[dim])
+    shape = [n * ways if d == dim else n for d, n in enumerate(value.shape)]
+    full = lax.dynamic_update_slice_in_dim(
+        jnp.zeros(shape, value.dtype), value, here * step, axis=dim
+    )
+    for far in range(1, ways):
+        value = lax.ppermute(value, axis, [(d, (d + 1) % ways) for d in range(ways)])
+        full = lax.dynamic_update_slice_in_dim(full, value, (here - far) % ways * step, axis=dim)
+    return full
 
 
 def unit_circle(numerator, modulus):
@@ -135,10 +147,7 @@
     )
     running_max, totals, weighted = absorb(
         initial,
-        (
-            lax.all_gather(key_rows, "ctx", axis=0, tiled=True),
-            lax.all_gather(value_rows, "ctx", axis=0, tiled=True),
-        ),
+        (ring_gather(key_rows, "ctx", 0), lax.all_gather(value_rows, "ctx", axis=0, tiled=True)),
         jnp.int32(0),
     )
     attended = (weighted / totals[:, None]).astype(jnp.bfloat16)

time: 392 us -> 480 us (1.22)
  waiting for transfers between devices: 187 us -> 277 us
  blocking collectives: 47.3 us -> 20.8 us
  local copies, waits for them, and re-layouts: 38.4 us -> 58.4 us
    ppermute x0 -> x15, waiting for transfers between devices: none -> 88.2 us  [ring_gather(): lax.ppermute(value, axis, [(d, (d + 1) % ways) for d in range(ways)])]
    all_gather x1 -> x0, blocking collectives: 28.5 us -> none  [per_device(): lax.all_gather(key_rows, 'ctx', axis=0, tiled=True)]
    dynamic_update_slice x0 -> x16, local copies, waits for them, and re-layouts: none -> 16.7 us  [the longest x15 15.2 us: ring_gather(): lax.dynamic_update_slice_in_dim(full, value, (here - far) % ways * step,...]
    unnamed x7 -> x15, local copies, waits for them, and re-layouts: 24.7 us -> 27.2 us
  transfers between devices with their start and end apart: 2 -> 17, of which waited for: 2 -> 16; matrix products, arithmetic and copies ran while one was open for 1% -> 1% of each run, Pallas kernels for 0% -> 0%
where the time goes in v1:
time: 480 us; the launch traced here: 475 us
  waiting for transfers between devices  277 us (58%)
  local copies, waits for them, and re-layouts  58.4 us (12%)
  starting transfers between devices  45.6 us (10%)
  matrix products  36.3 us (8%)
  other arithmetic  35.5 us (7%)
  blocking collectives  20.8 us (4%)
    all_to_all x1, waiting for transfers between devices, per_device(): lax.all_to_all(turned, 'ctx', split_axis=1, concat_axis=2, tiled=True)  150 us
    ppermute x15, waiting for transfers between devices, ring_gather(): lax.ppermute(value, axis, [(d, (d + 1) % ways) for d in range(ways)])  88.2 us
    all_to_all x1, waiting for transfers between devices, per_device(): lax.all_to_all(mixed_rows.reshape(axis_count, rows_dev, chan_count), 'ctx...  38.7 us
    all_to_all x1, starting transfers between devices, per_device(): lax.all_to_all(mixed_rows.reshape(axis_count, rows_dev, chan_count), 'ctx...  36.5 us
    unnamed x15, local copies, waits for them, and re-layouts  27.2 us
    all_gather x1, blocking collectives, per_device(): lax.all_gather(value_rows, 'ctx', axis=0, tiled=True)  20.8 us
    dynamic_update_slice x15, local copies, waits for them, and re-layouts, ring_gather(): lax.dynamic_update_slice_in_dim(full, value, (here - far) % ways * step,...  15.2 us
    sub x1, other arithmetic, per_device(): signal[0] * kernel[0] - signal[1] * kernel[1]  10.9 us
  transfers between devices with their start and end apart: 17, of which 16 were waited for; matrix products, arithmetic and copies ran while one was open for 1% of the time, Pallas kernels for 0%

profile of v1, /device:TPU:0, one launch (start us, length us, event | category | flops | bytes accessed | tf_op | source)
XLA Modules:
  0.0 474.7 jit_solution(5989156318004918940)
XLA Ops:
  0.0 11.3 %copy.21 = bf16[2,256,4096]{1,0,2:T(2,128)(2,1)} copy(bf16[2,256,4096]{2,1,0:T(8,128)(2,1)} %param.6) | data formatting | bytes 8388608 | tf_op args[0]
  11.3 6.7 %convert_element_type.58 = f32[2,256,4096]{1,0,2:T(2,128)} convert(bf16[2,256,4096]{1,0,2:T(2,128)(2,1)} %copy.21) | non-fusion elementwise | flops 2097152 | bytes 12582912 | tf_op jit(solution)/shard_map/convert_element_type | solution.py:71
  18.0 11.1 %copy.22 = bf16[2,256,4096]{1,0,2:T(2,128)(2,1)} copy(bf16[2,256,4096]{2,1,0:T(8,128)(2,1)} %param.7) | data formatting | bytes 8388608 | tf_op args[1]
  29.1 5.2 %convert_element_type.59 = f32[2,256,4096]{1,0,2:T(2,128)S(1)} convert(bf16[2,256,4096]{1,0,2:T(2,128)(2,1)} %copy.22) | non-fusion elementwise | flops 2097152 | bytes 12582912 | tf_op jit(solution)/shard_map/convert_element_type | solution.py:72
  34.3 10.9 %multiply_subtract_fusion = (f32[1,256,4096]{1,0,2:T(1,128)S(1)}, f32[1,256,4096]{1,0,2:T(1,128)S(1)}) fusion(f32[2,256,4096]{1,0,2:T(2,128)S(1)} %convert_element_type.59, f32[2,256,4096]{1,0,2:T(2,128)S(1)} %copy-done.1), kind=kLoop, calls=%fused_computation.46 | loop fusion | flops 6291456 | bytes 25165824 | tf_op jit(solution)/shard_map/sub | solution.py:75
  45.2 8.7 %maximum_bitcast_fusion = f32[2,4096,256]{2,0,1:T(2,128)} fusion(f32[1,256,4096]{1,0,2:T(1,128)S(1)} %get-tuple-element.1496, f32[1,256,4096]{1,0,2:T(1,128)S(1)} %get-tuple-element.1495), kind=kLoop, calls=%fused_computation.31 | loop fusion | flops 2097152 | bytes 16777216 | tf_op jit(solution)/shard_map/transpose | solution.py:80
  53.9 8.0 %all-to-all-start = ((f32[2,4096,256]{2,0,1:T(2,128)}), f32[2,4096,256]{2,0,1:T(2,128)}, u32[]{:S(2)}, u32[]{:S(2)}) async-start(f32[2,4096,256]{2,0,1:T(2,128)} %maximum_bitcast_fusion), calls=%async_computation | async-start | bytes 16777216 | tf_op jit(solution)/shard_map/all_to_all | solution.py:81
  62.0 150.0 %all-to-all-done = f32[2,4096,256]{2,0,1:T(2,128)} async-done(((f32[2,4096,256]{2,0,1:T(2,128)}), f32[2,4096,256]{2,0,1:T(2,128)}, u32[]{:S(2)}, u32[]{:S(2)}) %all-to-all-start) | async-done | bytes 8388640 | tf_op jit(solution)/shard_map/all_to_all | solution.py:81
  212.0 8.2 %copy.39 = f32[2,16,256,256]{3,1,2,0:T(8,128)S(1)} copy(f32[2,16,256,256]{3,0,2,1:T(2,128)} %bitcast.1) | data formatting | bytes 16777216 | tf_op jit(solution)/shard_map/all_to_all | solution.py:81
  224.3 4.3 fusion.18
  228.6 4.1 fusion.22
  232.7 5.1 %fusion.12 = (f32[256,16,256]{2,1,0:T(8,128)S(1)}, f32[256,16,256]{2,1,0:T(8,128)S(1)}) fusion(f32[256,256,16]{1,2,0:T(8,128)S(1)} %fusion.22, f32[16,256]{1,0:T(8,128)S(1)} %get-tuple-element.1501, f32[16,256]{1,0:T(8,128)S(1)} %get-tuple-element.1502, f32[256,256,16]{1,2,0:T(8,128)S(1)} %fusion.18, f32[2,256,16,256]{3,2,1,0:T(8,128)S(1)} %bitcast.74), kind=kOutput, calls=%fused_computation.37 | convolution fusion | flops 208670208 | bytes 21004288 | tf_op jit(solution)/shard_map/ud,cdp->cup/dot_general | solution.py:38
  237.8 7.4 %fusion.14 = f32[256,16,128]{0,2,1:T(8,128)S(1)} fusion(f32[256,16,256]{2,1,0:T(8,128)S(1)} %get-tuple-element.1498), kind=kOutput, calls=%fused_computation.41 | convolution fusion | flops 1611071488 | bytes 6291456 | tf_op jit(solution)/shard_map/vp,cup->vuc/dot_general | solution.py:56
  245.3 7.3 %multiply_bitcast_fusion = f32[128,16,256]{2,0,1:T(8,128)S(1)} fusion(f32[256,16,128]{0,2,1:T(8,128)S(1)} %fusion.14, f32[256,16,256]{2,1,0:T(8,128)S(1)} %get-tuple-element.1497), kind=kOutput, calls=%fused_computation.55 | convolution fusion | flops 1612120064 | bytes 8388608 | tf_op jit(solution)/shard_map/vp,cup->vuc/dot_general | solution.py:56
  255.1 36.5 %all-to-all-start.1 = ((f32[16,128,256]{2,1,0:T(8,128)}), f32[16,128,256]{2,1,0:T(8,128)}, u32[]{:S(2)}, u32[]{:S(2)}) async-start(f32[16,128,256]{2,1,0:T(8,128)} %bitcast.75), calls=%async_computation.1 | async-start | bytes 4194304 | tf_op jit(solution)/shard_map/all_to_all | solution.py:86
  293.9 38.7 %all-to-all-done.1 = f32[16,128,256]{2,1,0:T(8,128)} async-done(((f32[16,128,256]{2,1,0:T(8,128)}), f32[16,128,256]{2,1,0:T(8,128)}, u32[]{:S(2)}, u32[]{:S(2)}) %all-to-all-start.1) | async-done | bytes 2097184 | tf_op jit(solution)/shard_map/all_to_all | solution.py:86
  339.4 10.5 %collective-permute-done = bf16[128,128]{1,0:T(8,128)(2,1)S(1)} collective-permute-done((bf16[128,128]{1,0:T(8,128)(2,1)S(1)}, bf16[128,128]{1,0:T(8,128)(2,1)S(1)}, u32[]{:S(2)}, u32[]{:S(2)}) %collective-permute-start) | collective-permute-done | bytes 32800 | tf_op jit(solution)/shard_map/ppermute | solution.py:19
  349.9 6.0 %collective-permute-done.1 = bf16[128,128]{1,0:T(8,128)(2,1)S(1)} collective-permute-done((bf16[128,128]{1,0:T(8,128)(2,1)S(1)}, bf16[128,128]{1,0:T(8,128)(2,1)S(1)}, u32[]{:S(2)}, u32[]{:S(2)}) %collective-permute-start.1) | collective-permute-done | bytes 32800 | tf_op jit(solution)/shard_map/ppermute | solution.py:19
  355.9 6.0 %collective-permute-done.2 = bf16[128,128]{1,0:T(8,128)(2,1)S(1)} collective-permute-done((bf16[128,128]{1,0:T(8,128)(2,1)S(1)}, bf16[128,128]{1,0:T(8,128)(2,1)S(1)}, u32[]{:S(2)}, u32[]{:S(2)}) %collective-permute-start.2) | collective-permute-done | bytes 32800 | tf_op jit(solution)/shard_map/ppermute | solution.py:19
  361.9 6.0 %collective-permute-done.3 = bf16[128,128]{1,0:T(8,128)(2,1)S(1)} collective-permute-done((bf16[128,128]{1,0:T(8,128)(2,1)S(1)}, bf16[128,128]{1,0:T(8,128)(2,1)S(1)}, u32[]{:S(2)}, u32[]{:S(2)}) %collective-permute-start.3) | collective-permute-done | bytes 32800 | tf_op jit(solution)/shard_map/ppermute | solution.py:19
  368.0 6.0 %collective-permute-done.4 = bf16[128,128]{1,0:T(8,128)(2,1)S(1)} collective-permute-done((bf16[128,128]{1,0:T(8,128)(2,1)S(1)}, bf16[128,128]{1,0:T(8,128)(2,1)S(1)}, u32[]{:S(2)}, u32[]{:S(2)}) %collective-permute-start.4) | collective-permute-done | bytes 32800 | tf_op jit(solution)/shard_map/ppermute | solution.py:19
  374.0 6.0 %collective-permute-done.5 = bf16[128,128]{1,0:T(8,128)(2,1)S(1)} collective-permute-done((bf16[128,128]{1,0:T(8,128)(2,1)S(1)}, bf16[128,128]{1,0:T(8,128)(2,1)S(1)}, u32[]{:S(2)}, u32[]{:S(2)}) %collective-permute-start.5) | collective-permute-done | bytes 32800 | tf_op jit(solution)/shard_map/ppermute | solution.py:19
  380.1 6.0 %collective-permute-done.6 = bf16[128,128]{1,0:T(8,128)(2,1)S(1)} collective-permute-done((bf16[128,128]{1,0:T(8,128)(2,1)S(1)}, bf16[128,128]{1,0:T(8,128)(2,1)S(1)}, u32[]{:S(2)}, u32[]{:S(2)}) %collective-permute-start.6) | collective-permute-done | bytes 32800 | tf_op jit(solution)/shard_map/ppermute | solution.py:19
  386.1 6.0 %collective-permute-done.7 = bf16[128,128]{1,0:T(8,128)(2,1)S(1)} collective-permute-done((bf16[128,128]{1,0:T(8,128)(2,1)S(1)}, bf16[128,128]{1,0:T(8,128)(2,1)S(1)}, u32[]{:S(2)}, u32[]{:S(2)}) %collective-permute-start.7) | collective-permute-done | bytes 32800 | tf_op jit(solution)/shard_map/ppermute | solution.py:19
  392.7 6.0 %collective-permute-done.8 = bf16[128,128]{1,0:T(8,128)(2,1)S(1)} collective-permute-done((bf16[128,128]{1,0:T(8,128)(2,1)S(1)}, bf16[128,128]{1,0:T(8,128)(2,1)S(1)}, u32[]{:S(2)}, u32[]{:S(2)}) %collective-permute-start.8) | collective-permute-done | bytes 32800 | tf_op jit(solution)/shard_map/ppermute | solution.py:19
  399.4 6.0 %collective-permute-done.9 = bf16[128,128]{1,0:T(8,128)(2,1)S(1)} collective-permute-done((bf16[128,128]{1,0:T(8,128)(2,1)S(1)}, bf16[128,128]{1,0:T(8,128)(2,1)S(1)}, u32[]{:S(2)}, u32[]{:S(2)}) %collective-permute-start.9) | collective-permute-done | bytes 32800 | tf_op jit(solution)/shard_map/ppermute | solution.py:19
  406.0 6.0 %collective-permute-done.10 = bf16[128,128]{1,0:T(8,128)(2,1)S(1)} collective-permute-done((bf16[128,128]{1,0:T(8,128)(2,1)S(1)}, bf16[128,128]{1,0:T(8,128)(2,1)S(1)}, u32[]{:S(2)}, u32[]{:S(2)}) %collective-permute-start.10) | collective-permute-done | bytes 32800 | tf_op jit(solution)/shard_map/ppermute | solution.py:19
  412.7 6.1 %collective-permute-done.11 = bf16[128,128]{1,0:T(8,128)(2,1)} collective-permute-done((bf16[128,128]{1,0:T(8,128)(2,1)S(1)}, bf16[128,128]{1,0:T(8,128)(2,1)}, u32[]{:S(2)}, u32[]{:S(2)}) %collective-permute-start.11) | collective-permute-done | bytes 32800 | tf_op jit(solution)/shard_map/ppermute | solution.py:19
  418.8 6.3 %collective-permute-done.12 = bf16[128,128]{1,0:T(8,128)(2,1)} collective-permute-done((bf16[128,128]{1,0:T(8,128)(2,1)}, bf16[128,128]{1,0:T(8,128)(2,1)}, u32[]{:S(2)}, u32[]{:S(2)}) %collective-permute-start.12) | collective-permute-done | bytes 32800 | tf_op jit(solution)/shard_map/ppermute | solution.py:19
  426.6 4.9 %collective-permute-done.13 = bf16[128,128]{1,0:T(8,128)(2,1)} collective-permute-done((bf16[128,128]{1,0:T(8,128)(2,1)}, bf16[128,128]{1,0:T(8,128)(2,1)}, u32[]{:S(2)}, u32[]{:S(2)}) %collective-permute-start.13) | collective-permute-done | bytes 32800 | tf_op jit(solution)/shard_map/ppermute | solution.py:19
  431.5 20.8 %all_gather.3 = bf16[2048,128]{1,0:T(8,128)(2,1)} all-gather(bf16[128,128]{1,0:T(8,128)(2,1)S(1)} %get-tuple-element.1499), channel_id=1, replica_groups=mesh['groups'=2,'ctx'=16] {'ctx'}, dimensions={0}, use_global_device_ids=true | all-gather | bytes 557056 | tf_op jit(solution)/shard_map/all_gather | solution.py:150
  452.4 21.3 %conditional.1 = (f32[128]{0:T(128)S(1)}, f32[128,128]{1,0:T(8,128)S(1)}) conditional(s32[]{:T(128)} %convert_element_type.57, (s32[2048]{0:T(1024)S(1)}, s32[128]{0:T(128)S(1)}, s32[]{:T(128)}, bf16[128,128]{1,0:T(8,128)(2,1)S(1)}, s32[]{:T(128)}, /*index=5*/bf16[128,128]{1,0:T(8,128)(2,1)S(1)}, s32[]{:T(128)}, ...), branch_computations={%region_1.4_spmd.clone.clone, %region_4.5_spmd} | conditional | flops 137380464 | bytes 5899837 | solution.py:124
  (62 shorter events, 40.9 us)
Async XLA Ops:
  0.0 337.6 %copy-start = (bf16[4096,384]{1,0:T(8,128)(2,1)S(1)}, bf16[4096,384]{1,0:T(8,128)(2,1)}, u32[]{:S(2)}) copy-start(bf16[4096,384]{1,0:T(8,128)(2,1)} %param.9) | copy-start | bytes 9437188
  29.1 5.2 %copy-start.1 = (f32[2,256,4096]{1,0,2:T(2,128)S(1)}, f32[2,256,4096]{1,0,2:T(2,128)}, u32[]{:S(2)}) copy-start(f32[2,256,4096]{1,0,2:T(2,128)} %convert_element_type.58) | copy-start | bytes 25165828
  53.9 158.0 %all-to-all-start = ((f32[2,4096,256]{2,0,1:T(2,128)}), f32[2,4096,256]{2,0,1:T(2,128)}, u32[]{:S(2)}, u32[]{:S(2)}) async-start(f32[2,4096,256]{2,0,1:T(2,128)} %maximum_bitcast_fusion), calls=%async_computation | async-start | bytes 16777216 | tf_op jit(solution)/shard_map/all_to_all | solution.py:81
  255.1 77.6 %all-to-all-start.1 = ((f32[16,128,256]{2,1,0:T(8,128)}), f32[16,128,256]{2,1,0:T(8,128)}, u32[]{:S(2)}, u32[]{:S(2)}) async-start(f32[16,128,256]{2,1,0:T(8,128)} %bitcast.75), calls=%async_computation.1 | async-start | bytes 4194304 | tf_op jit(solution)/shard_map/all_to_all | solution.py:86
  338.4 11.5 %collective-permute-start = (bf16[128,128]{1,0:T(8,128)(2,1)S(1)}, bf16[128,128]{1,0:T(8,128)(2,1)S(1)}, u32[]{:S(2)}, u32[]{:S(2)}) collective-permute-start(bf16[128,128]{1,0:T(8,128)(2,1)S(1)} %get-tuple-element.1500), channel_id=1, source_target_pairs={{0,1},{1,2},{2,3},{3,4},{4,5},{5,6},{6,7},{7,8},{8,9},{9,10},{10,1... | collective-permute-start | bytes 98312 | tf_op jit(solution)/shard_map/ppermute | solution.py:19
  349.9 6.0 %collective-permute-start.1 = (bf16[128,128]{1,0:T(8,128)(2,1)S(1)}, bf16[128,128]{1,0:T(8,128)(2,1)S(1)}, u32[]{:S(2)}, u32[]{:S(2)}) collective-permute-start(bf16[128,128]{1,0:T(8,128)(2,1)S(1)} %collective-permute-done), channel_id=1, source_target_pairs={{0,1},{1,2},{2,3},{3,4},{4,5},{5,6},{6,7},{7,8},{8,9},{9,10},{10,1... | collective-permute-start | bytes 98312 | tf_op jit(solution)/shard_map/ppermute | solution.py:19
  355.9 6.0 %collective-permute-start.2 = (bf16[128,128]{1,0:T(8,128)(2,1)S(1)}, bf16[128,128]{1,0:T(8,128)(2,1)S(1)}, u32[]{:S(2)}, u32[]{:S(2)}) collective-permute-start(bf16[128,128]{1,0:T(8,128)(2,1)S(1)} %collective-permute-done.1), channel_id=1, source_target_pairs={{0,1},{1,2},{2,3},{3,4},{4,5},{5,6},{6,7},{7,8},{8,9},{9,10},{10,1... | collective-permute-start | bytes 98312 | tf_op jit(solution)/shard_map/ppermute | solution.py:19
  361.9 6.0 %collective-permute-start.3 = (bf16[128,128]{1,0:T(8,128)(2,1)S(1)}, bf16[128,128]{1,0:T(8,128)(2,1)S(1)}, u32[]{:S(2)}, u32[]{:S(2)}) collective-permute-start(bf16[128,128]{1,0:T(8,128)(2,1)S(1)} %collective-permute-done.2), channel_id=1, source_target_pairs={{0,1},{1,2},{2,3},{3,4},{4,5},{5,6},{6,7},{7,8},{8,9},{9,10},{10,1... | collective-permute-start | bytes 98312 | tf_op jit(solution)/shard_map/ppermute | solution.py:19
  368.0 6.0 %collective-permute-start.4 = (bf16[128,128]{1,0:T(8,128)(2,1)S(1)}, bf16[128,128]{1,0:T(8,128)(2,1)S(1)}, u32[]{:S(2)}, u32[]{:S(2)}) collective-permute-start(bf16[128,128]{1,0:T(8,128)(2,1)S(1)} %collective-permute-done.3), channel_id=1, source_target_pairs={{0,1},{1,2},{2,3},{3,4},{4,5},{5,6},{6,7},{7,8},{8,9},{9,10},{10,1... | collective-permute-start | bytes 98312 | tf_op jit(solution)/shard_map/ppermute | solution.py:19
  374.0 6.0 %collective-permute-start.5 = (bf16[128,128]{1,0:T(8,128)(2,1)S(1)}, bf16[128,128]{1,0:T(8,128)(2,1)S(1)}, u32[]{:S(2)}, u32[]{:S(2)}) collective-permute-start(bf16[128,128]{1,0:T(8,128)(2,1)S(1)} %collective-permute-done.4), channel_id=1, source_target_pairs={{0,1},{1,2},{2,3},{3,4},{4,5},{5,6},{6,7},{7,8},{8,9},{9,10},{10,1... | collective-permute-start | bytes 98312 | tf_op jit(solution)/shard_map/ppermute | solution.py:19
  380.0 6.0 %collective-permute-start.6 = (bf16[128,128]{1,0:T(8,128)(2,1)S(1)}, bf16[128,128]{1,0:T(8,128)(2,1)S(1)}, u32[]{:S(2)}, u32[]{:S(2)}) collective-permute-start(bf16[128,128]{1,0:T(8,128)(2,1)S(1)} %collective-permute-done.5), channel_id=1, source_target_pairs={{0,1},{1,2},{2,3},{3,4},{4,5},{5,6},{6,7},{7,8},{8,9},{9,10},{10,1... | collective-permute-start | bytes 98312 | tf_op jit(solution)/shard_map/ppermute | solution.py:19
  386.1 6.0 %collective-permute-start.7 = (bf16[128,128]{1,0:T(8,128)(2,1)S(1)}, bf16[128,128]{1,0:T(8,128)(2,1)S(1)}, u32[]{:S(2)}, u32[]{:S(2)}) collective-permute-start(bf16[128,128]{1,0:T(8,128)(2,1)S(1)} %collective-permute-done.6), channel_id=1, source_target_pairs={{0,1},{1,2},{2,3},{3,4},{4,5},{5,6},{6,7},{7,8},{8,9},{9,10},{10,1... | collective-permute-start | bytes 98312 | tf_op jit(solution)/shard_map/ppermute | solution.py:19
  392.1 0.6 copy-start.2
  392.7 6.0 %collective-permute-start.8 = (bf16[128,128]{1,0:T(8,128)(2,1)S(1)}, bf16[128,128]{1,0:T(8,128)(2,1)S(1)}, u32[]{:S(2)}, u32[]{:S(2)}) collective-permute-start(bf16[128,128]{1,0:T(8,128)(2,1)S(1)} %collective-permute-done.7), channel_id=1, source_target_pairs={{0,1},{1,2},{2,3},{3,4},{4,5},{5,6},{6,7},{7,8},{8,9},{9,10},{10,1... | collective-permute-start | bytes 98312 | tf_op jit(solution)/shard_map/ppermute | solution.py:19
  398.8 0.6 copy-start.3
  399.4 6.0 %collective-permute-start.9 = (bf16[128,128]{1,0:T(8,128)(2,1)S(1)}, bf16[128,128]{1,0:T(8,128)(2,1)S(1)}, u32[]{:S(2)}, u32[]{:S(2)}) collective-permute-start(bf16[128,128]{1,0:T(8,128)(2,1)S(1)} %collective-permute-done.8), channel_id=1, source_target_pairs={{0,1},{1,2},{2,3},{3,4},{4,5},{5,6},{6,7},{7,8},{8,9},{9,10},{10,1... | collective-permute-start | bytes 98312 | tf_op jit(solution)/shard_map/ppermute | solution.py:19
  405.4 0.6 copy-start.4
  406.0 6.0 %collective-permute-start.10 = (bf16[128,128]{1,0:T(8,128)(2,1)S(1)}, bf16[128,128]{1,0:T(8,128)(2,1)S(1)}, u32[]{:S(2)}, u32[]{:S(2)}) collective-permute-start(bf16[128,128]{1,0:T(8,128)(2,1)S(1)} %collective-permute-done.9), channel_id=1, source_target_pairs={{0,1},{1,2},{2,3},{3,4},{4,5},{5,6},{6,7},{7,8},{8,9},{9,10},{10,1... | collective-permute-start | bytes 98312 | tf_op jit(solution)/shard_map/ppermute | solution.py:19
  412.1 0.6 copy-start.5
  412.7 6.1 %collective-permute-start.11 = (bf16[128,128]{1,0:T(8,128)(2,1)S(1)}, bf16[128,128]{1,0:T(8,128)(2,1)}, u32[]{:S(2)}, u32[]{:S(2)}) collective-permute-start(bf16[128,128]{1,0:T(8,128)(2,1)S(1)} %collective-permute-done.10), channel_id=1, source_target_pairs={{0,1},{1,2},{2,3},{3,4},{4,5},{5,6},{6,7},{7,8},{8,9},{9,10},{10,1... | collective-permute-start | bytes 98312 | tf_op jit(solution)/shard_map/ppermute | solution.py:19
  418.8 6.4 %collective-permute-start.12 = (bf16[128,128]{1,0:T(8,128)(2,1)}, bf16[128,128]{1,0:T(8,128)(2,1)}, u32[]{:S(2)}, u32[]{:S(2)}) collective-permute-start(bf16[128,128]{1,0:T(8,128)(2,1)} %collective-permute-done.11), channel_id=1, source_target_pairs={{0,1},{1,2},{2,3},{3,4},{4,5},{5,6},{6,7},{7,8},{8,9},{9,10},{10,1... | collective-permute-start | bytes 98312 | tf_op jit(solution)/shard_map/ppermute | solution.py:19
  425.2 6.4 %collective-permute-start.13 = (bf16[128,128]{1,0:T(8,128)(2,1)}, bf16[128,128]{1,0:T(8,128)(2,1)}, u32[]{:S(2)}, u32[]{:S(2)}) collective-permute-start(bf16[128,128]{1,0:T(8,128)(2,1)} %collective-permute-done.12), channel_id=1, source_target_pairs={{0,1},{1,2},{2,3},{3,4},{4,5},{5,6},{6,7},{7,8},{8,9},{9,10},{10,1... | collective-permute-start | bytes 98312 | tf_op jit(solution)/shard_map/ppermute | solution.py:19
  431.5 20.8 %collective-permute-start.14 = (bf16[128,128]{1,0:T(8,128)(2,1)}, bf16[128,128]{1,0:T(8,128)(2,1)}, u32[]{:S(2)}, u32[]{:S(2)}) collective-permute-start(bf16[128,128]{1,0:T(8,128)(2,1)} %collective-permute-done.13), channel_id=1, source_target_pairs={{0,1},{1,2},{2,3},{3,4},{4,5},{5,6},{6,7},{7,8},{8,9},{9,10},{10,1... | collective-permute-start | bytes 98312 | tf_op jit(solution)/shard_map/ppermute | solution.py:19
